TPU v7x, 256 devices: a whole 4x4x8 slice. The times are simulated.
256 devices in a mesh: row: 16 (over x_hi, y, core), col: 16 (over x_lo, z).
Axes of the slice: x: 4 (x_hi: 2, x_lo: 2; x = x_hi * 2 + x_lo), y: 4, z: 8, core: 2. Of those that a mesh axis runs over, the one named last changes fastest.
Arguments:
- video_rows: bfloat16 [98304, 1024], P(('row', 'col')), may hold values from -1.5 to 1.5
- video_ids: int32 [98304], P(('row', 'col')), may hold values from 0 to 767
- imu_rows: bfloat16 [98304, 1024], P(('row', 'col')), may hold values from -1.5 to 1.5
- imu_ids: int32 [98304], P(('row', 'col')), may hold values from 0 to 767
- audio_rows: bfloat16 [98304, 1024], P(('row', 'col')), may hold values from -1.5 to 1.5
- audio_ids: int32 [98304], P(('row', 'col')), may hold values from 0 to 767
- imu_log_scale: float32 [1], replicated, may hold values from 0 to 1
- imu_bias: float32 [1], replicated, may hold values from -3 to -1
- audio_log_scale: float32 [1], replicated, may hold values from 0 to 1
- audio_bias: float32 [1], replicated, may hold values from -3 to -1
Outputs:
- video_grad: float32 [98304, 1024], P(('row', 'col'))
- imu_grad: float32 [98304, 1024], P(('row', 'col'))
- audio_grad: float32 [98304, 1024], P(('row', 'col'))
- row_loss: float32 [98304], P(('row', 'col'))
All inputs are finite; a program needn't handle non-finite values.
Results may differ from a plain program's by a relative error of at most 0.0025.
Values may be sent and summed in bfloat16 or wider, within the bound.
A program may use at most 128 MiB of HBM per device.

v0:
```python
import jax
import jax.numpy as jnp
from jax import lax
from jax.sharding import PartitionSpec as P

STEPS = 4


def passed_along(shard, axis, by):
    devices = lax.axis_size(axis)
    return lax.ppermute(shard, axis, [(i, (i + by) % devices) for i in range(devices)])


def weight_tile(video_block, video_tags, partner, partner_tags, scale, offset):
    products = lax.dot_general(
        video_block, partner, (((1,), (1,)), ((), ())), preferred_element_type=jnp.float32
    )
    logits = scale * products + offset
    signs = jnp.where(video_tags[:, None] == partner_tags[None, :], 1.0, -1.0).astype(logits.dtype)
    losses = jax.nn.softplus(-signs * logits)
    weighted = (-signs * jax.nn.sigmoid(-signs * logits) * scale).astype(jnp.bfloat16)
    return (losses, weighted)


def pair_tile(video_block, video_tags, partner, partner_tags, scale, offset):
    losses, weighted = weight_tile(video_block, video_tags, partner, partner_tags, scale, offset)
    video_term = jnp.dot(weighted, partner, preferred_element_type=jnp.float32)
    partner_term = lax.dot_general(
        weighted, video_block, (((0,), (0,)), ((), ())), preferred_element_type=jnp.float32
    )
    return (jnp.sum(losses, axis=1), video_term, partner_term)


def per_device(
    video_rows,
    video_ids,
    imu_rows,
    imu_ids,
    audio_rows,
    audio_ids,
    imu_log_scale,
    imu_bias,
    audio_log_scale,
    audio_bias,
):
    scale_imu = jnp.exp(imu_log_scale[0])
    scale_audio = jnp.exp(audio_log_scale[0])
    offset_imu = imu_bias[0]
    offset_audio = audio_bias[0]
    rows_here = video_rows.shape[0]
    width = video_rows.shape[1]
    imu_block, imu_tags = (imu_rows, imu_ids)
    audio_block, audio_tags = (audio_rows, audio_ids)
    loss_sum = jnp.zeros((rows_here,), jnp.float32)
    video_acc = jnp.zeros((rows_here, width), jnp.float32)
    imu_acc = jnp.zeros((rows_here, width), jnp.float32)
    audio_acc = jnp.zeros((rows_here, width), jnp.float32)
    for rotation in range(STEPS):
        if rotation > 0:
            imu_block, imu_tags = passed_along((imu_block, imu_tags), "row", 1)
            audio_block, audio_tags = passed_along((audio_block, audio_tags), "col", 1)
        loss_imu, video_imu, imu_term = pair_tile(
            video_rows, video_ids, imu_block, imu_tags, scale_imu, offset_imu
        )
        loss_audio, video_audio, audio_term = pair_tile(
            video_rows, video_ids, audio_block, audio_tags, scale_audio, offset_audio
        )
        loss_sum = loss_sum + (loss_imu + loss_audio)
        video_acc = video_acc + (video_imu + video_audio)
        imu_acc = imu_acc + imu_term
        audio_acc = audio_acc + audio_term
        if rotation < STEPS - 1:
            imu_acc = passed_along(imu_acc, "row", 1)
            audio_acc = passed_along(audio_acc, "col", 1)
        else:
            imu_acc = passed_along(imu_acc, "row", -(STEPS - 1))
            audio_acc = passed_along(audio_acc, "col", -(STEPS - 1))
    row_loss = loss_sum / (2.0 * STEPS * rows_here)
    return (video_acc, imu_acc, audio_acc, row_loss)


def solution(mesh):
    in_specs = (
        P(("row", "col"), None),
        P(("row", "col")),
        P(("row", "col"), None),
        P(("row", "col")),
        P(("row", "col"), None),
        P(("row", "col")),
        P(),
        P(),
        P(),
        P(),
    )
    out_specs = (
        P(("row", "col"), None),
        P(("row", "col"), None),
        P(("row", "col"), None),
        P(("row", "col")),
    )
    return jax.shard_map(
        per_device, mesh=mesh, in_specs=in_specs, out_specs=out_specs, check_vma=False
    )
```

profile of v0, /device:TPU:9, one launch (start us, length us, event | category | flops | bytes accessed | tf_op | source)
XLA Modules:
  0.0 343.6 jit_solution(16790690157812337406)
XLA Ops:
  0.6 1.7 collective-permute-start.3
  3.7 2.1 fusion.16
  6.6 2.2 collective-permute-start.12
  10.1 0.9 fusion.17
  11.8 1.7 collective-permute-start.16
  13.8 1.6 collective-permute-start.2
  15.4 43.0 %collective-permute-done.2 = s32[384]{0:T(512)S(1)} collective-permute-done((s32[384]{0:T(512)S(1)}, s32[384]{0:T(512)S(1)}, u32[]{:S(2)}, u32[]{:S(2)}) %collective-permute-start.2) | collective-permute-done | bytes 1568 | tf_op jit(solution)/shard_map/ppermute | solution.py:11
  58.5 2.4 collective-permute-start
  60.9 0.9 fusion.19
  61.8 0.9 fusion.18
  63.5 2.2 collective-permute-start.13
  67.5 47.8 %collective-permute-done.6 = s32[384]{0:T(512)S(1)} collective-permute-done((s32[384]{0:T(512)S(1)}, s32[384]{0:T(512)S(1)}, u32[]{:S(2)}, u32[]{:S(2)}) %collective-permute-start.6) | collective-permute-done | bytes 1568 | tf_op jit(solution)/shard_map/ppermute | solution.py:11
  115.3 1.4 collective-permute-start.4
  116.7 0.9 fusion.21
  117.6 0.9 fusion.20
  119.3 2.1 collective-permute-start.14
  122.2 0.8 fusion.27
  123.1 20.9 %collective-permute-start.9 = (bf16[384,1024]{1,0:T(8,128)(2,1)S(1)}, bf16[384,1024]{1,0:T(8,128)(2,1)S(1)}, u32[]{:S(2)}, u32[]{:S(2)}) collective-permute-start(bf16[384,1024]{1,0:T(8,128)(2,1)S(1)} %collective-permute-done.5), channel_id=1, source_target_pairs={{0,16},{16,32},{32,48},{48,64},{64,80},{80,96},{96,112},{112,128},... | collective-permute-start | bytes 2359304 | tf_op jit(solution)/shard_map/ppermute | solution.py:11
  144.0 0.8 fusion.28
  144.8 0.8 fusion.29
  145.5 25.9 %collective-permute-done.10 = s32[384]{0:T(512)S(1)} collective-permute-done((s32[384]{0:T(512)S(1)}, s32[384]{0:T(512)S(1)}, u32[]{:S(2)}, u32[]{:S(2)}) %collective-permute-start.10) | collective-permute-done | bytes 1568 | tf_op jit(solution)/shard_map/ppermute | solution.py:11
  171.4 11.2 %collective-permute-start.8 = (s32[384]{0:T(512)S(1)}, s32[384]{0:T(512)S(1)}, u32[]{:S(2)}, u32[]{:S(2)}) collective-permute-start(s32[384]{0:T(512)S(1)} %collective-permute-done.4), channel_id=1, source_target_pairs={{0,16},{16,32},{32,48},{48,64},{64,80},{80,96},{96,112},{112,128},... | collective-permute-start | bytes 4616 | tf_op jit(solution)/shard_map/ppermute | solution.py:11
  182.6 0.9 fusion.23
  183.5 0.9 fusion.22
  185.2 80.3 %collective-permute-start.15 = (f32[384,1024]{1,0:T(8,128)S(1)}, f32[384,1024]{1,0:T(8,128)S(1)}, u32[]{:S(2)}, u32[]{:S(2)}) collective-permute-start(f32[384,1024]{1,0:T(8,128)S(1)} %fusion.37), channel_id=1, source_target_pairs={{0,208},{16,224},{32,240},{48,0},{64,16},{80,32},{96,48},{112,64},... | collective-permute-start | bytes 4718600 | tf_op jit(solution)/shard_map/ppermute | solution.py:11
  266.2 0.7 fusion.31
  268.3 0.7 fusion.39
  269.1 2.2 add_add_fusion
  271.3 27.2 %collective-permute-done.15 = f32[384,1024]{1,0:T(8,128)S(1)} collective-permute-done((f32[384,1024]{1,0:T(8,128)S(1)}, f32[384,1024]{1,0:T(8,128)S(1)}, u32[]{:S(2)}, u32[]{:S(2)}) %collective-permute-start.15) | collective-permute-done | bytes 1572896 | tf_op jit(solution)/shard_map/ppermute | solution.py:11
  298.4 42.9 %collective-permute-done.19 = f32[384,1024]{1,0:T(8,128)S(1)} collective-permute-done((f32[384,1024]{1,0:T(8,128)S(1)}, f32[384,1024]{1,0:T(8,128)S(1)}, u32[]{:S(2)}, u32[]{:S(2)}) %collective-permute-start.19) | collective-permute-done | bytes 1572896 | tf_op jit(solution)/shard_map/ppermute | solution.py:11
  341.3 1.1 copy.20
  342.5 1.1 copy.21
  (47 shorter events, 8.7 us)
Async XLA Ops:
  0.6 3.1 copy-start
  0.6 60.2 %collective-permute-start.3 = (bf16[384,1024]{1,0:T(8,128)(2,1)}, bf16[384,1024]{1,0:T(8,128)(2,1)S(1)}, u32[]{:S(2)}, u32[]{:S(2)}) collective-permute-start(bf16[384,1024]{1,0:T(8,128)(2,1)} %param.14), channel_id=1, source_target_pairs={{0,1},{1,2},{2,3},{3,4},{4,5},{5,6},{6,7},{7,8},{8,9},{9,10},{10,1... | collective-permute-start | bytes 2359304 | tf_op jit(solution)/shard_map/ppermute | solution.py:11
  3.7 2.1 copy-start.1
  3.7 2.1 copy-start.4
  5.8 4.3 %copy-start.3 = (bf16[384,1024]{1,0:T(8,128)(2,1)S(1)}, bf16[384,1024]{1,0:T(8,128)(2,1)}, u32[]{:S(2)}) copy-start(bf16[384,1024]{1,0:T(8,128)(2,1)} %param.14) | copy-start | bytes 2359300
  5.8 4.3 %copy-start.5 = (s32[384]{0:T(512)S(1)}, s32[384]{0:T(512)}, u32[]{:S(2)}) copy-start(s32[384]{0:T(512)} %param.15) | copy-start | bytes 4612
  6.6 56.2 %collective-permute-start.12 = (f32[384,1024]{1,0:T(8,128)S(1)}, f32[384,1024]{1,0:T(8,128)S(1)}, u32[]{:S(2)}, u32[]{:S(2)}) collective-permute-start(f32[384,1024]{1,0:T(8,128)S(1)} %fusion.24), channel_id=1, source_target_pairs={{0,16},{16,32},{32,48},{48,64},{64,80},{80,96},{96,112},{112,128},... | collective-permute-start | bytes 4718600 | tf_op jit(solution)/shard_map/ppermute | solution.py:11
  11.0 2.4 copy-start.2
  11.8 53.9 %collective-permute-start.16 = (f32[384,1024]{1,0:T(8,128)S(1)}, f32[384,1024]{1,0:T(8,128)S(1)}, u32[]{:S(2)}, u32[]{:S(2)}) collective-permute-start(f32[384,1024]{1,0:T(8,128)S(1)} %fusion.26), channel_id=1, source_target_pairs={{0,1},{1,2},{2,3},{3,4},{4,5},{5,6},{6,7},{7,8},{8,9},{9,10},{10,1... | collective-permute-start | bytes 4718600 | tf_op jit(solution)/shard_map/ppermute | solution.py:11
  13.5 48.3 %collective-permute-start.1 = (bf16[384,1024]{1,0:T(8,128)(2,1)S(1)}, bf16[384,1024]{1,0:T(8,128)(2,1)S(1)}, u32[]{:S(2)}, u32[]{:S(2)}) collective-permute-start(bf16[384,1024]{1,0:T(8,128)(2,1)S(1)} %copy-done.2), channel_id=1, source_target_pairs={{0,16},{16,32},{32,48},{48,64},{64,80},{80,96},{96,112},{112,128},... | collective-permute-start | bytes 2359304 | tf_op jit(solution)/shard_map/ppermute | solution.py:11
  13.8 44.7 %collective-permute-start.2 = (s32[384]{0:T(512)S(1)}, s32[384]{0:T(512)S(1)}, u32[]{:S(2)}, u32[]{:S(2)}) collective-permute-start(s32[384]{0:T(512)S(1)} %copy-done.5), channel_id=1, source_target_pairs={{0,1},{1,2},{2,3},{3,4},{4,5},{5,6},{6,7},{7,8},{8,9},{9,10},{10,1... | collective-permute-start | bytes 4616 | tf_op jit(solution)/shard_map/ppermute | solution.py:11
  58.5 3.3 collective-permute-start
  60.9 55.8 %collective-permute-start.7 = (bf16[384,1024]{1,0:T(8,128)(2,1)S(1)}, bf16[384,1024]{1,0:T(8,128)(2,1)S(1)}, u32[]{:S(2)}, u32[]{:S(2)}) collective-permute-start(bf16[384,1024]{1,0:T(8,128)(2,1)S(1)} %collective-permute-done.3), channel_id=1, source_target_pairs={{0,1},{1,2},{2,3},{3,4},{4,5},{5,6},{6,7},{7,8},{8,9},{9,10},{10,1... | collective-permute-start | bytes 2359304 | tf_op jit(solution)/shard_map/ppermute | solution.py:11
  63.5 55.1 %collective-permute-start.13 = (f32[384,1024]{1,0:T(8,128)S(1)}, f32[384,1024]{1,0:T(8,128)S(1)}, u32[]{:S(2)}, u32[]{:S(2)}) collective-permute-start(f32[384,1024]{1,0:T(8,128)S(1)} %convolution_add_fusion.1), channel_id=1, source_target_pairs={{0,16},{16,32},{32,48},{48,64},{64,80},{80,96},{96,112},{112,128},... | collective-permute-start | bytes 4718600 | tf_op jit(solution)/shard_map/ppermute | solution.py:11
  66.3 55.1 %collective-permute-start.17 = (f32[384,1024]{1,0:T(8,128)S(1)}, f32[384,1024]{1,0:T(8,128)S(1)}, u32[]{:S(2)}, u32[]{:S(2)}) collective-permute-start(f32[384,1024]{1,0:T(8,128)S(1)} %convolution_add_fusion), channel_id=1, source_target_pairs={{0,1},{1,2},{2,3},{3,4},{4,5},{5,6},{6,7},{7,8},{8,9},{9,10},{10,1... | collective-permute-start | bytes 4718600 | tf_op jit(solution)/shard_map/ppermute | solution.py:11
  66.6 51.0 %collective-permute-start.5 = (bf16[384,1024]{1,0:T(8,128)(2,1)S(1)}, bf16[384,1024]{1,0:T(8,128)(2,1)S(1)}, u32[]{:S(2)}, u32[]{:S(2)}) collective-permute-start(bf16[384,1024]{1,0:T(8,128)(2,1)S(1)} %collective-permute-done.1), channel_id=1, source_target_pairs={{0,16},{16,32},{32,48},{48,64},{64,80},{80,96},{96,112},{112,128},... | collective-permute-start | bytes 2359304 | tf_op jit(solution)/shard_map/ppermute | solution.py:11
  66.7 48.6 %collective-permute-start.6 = (s32[384]{0:T(512)S(1)}, s32[384]{0:T(512)S(1)}, u32[]{:S(2)}, u32[]{:S(2)}) collective-permute-start(s32[384]{0:T(512)S(1)} %collective-permute-done.2), channel_id=1, source_target_pairs={{0,1},{1,2},{2,3},{3,4},{4,5},{5,6},{6,7},{7,8},{8,9},{9,10},{10,1... | collective-permute-start | bytes 4616 | tf_op jit(solution)/shard_map/ppermute | solution.py:11
  115.3 2.3 collective-permute-start.4
  116.7 65.9 %collective-permute-start.11 = (bf16[384,1024]{1,0:T(8,128)(2,1)S(1)}, bf16[384,1024]{1,0:T(8,128)(2,1)S(1)}, u32[]{:S(2)}, u32[]{:S(2)}) collective-permute-start(bf16[384,1024]{1,0:T(8,128)(2,1)S(1)} %collective-permute-done.7), channel_id=1, source_target_pairs={{0,1},{1,2},{2,3},{3,4},{4,5},{5,6},{6,7},{7,8},{8,9},{9,10},{10,1... | collective-permute-start | bytes 2359304 | tf_op jit(solution)/shard_map/ppermute | solution.py:11
  119.3 65.1 %collective-permute-start.14 = (f32[384,1024]{1,0:T(8,128)S(1)}, f32[384,1024]{1,0:T(8,128)S(1)}, u32[]{:S(2)}, u32[]{:S(2)}) collective-permute-start(f32[384,1024]{1,0:T(8,128)S(1)} %fusion.32), channel_id=1, source_target_pairs={{0,16},{16,32},{32,48},{48,64},{64,80},{80,96},{96,112},{112,128},... | collective-permute-start | bytes 4718600 | tf_op jit(solution)/shard_map/ppermute | solution.py:11
  122.1 143.3 %collective-permute-start.18 = (f32[384,1024]{1,0:T(8,128)S(1)}, f32[384,1024]{1,0:T(8,128)S(1)}, u32[]{:S(2)}, u32[]{:S(2)}) collective-permute-start(f32[384,1024]{1,0:T(8,128)S(1)} %fusion.35), channel_id=1, source_target_pairs={{0,1},{1,2},{2,3},{3,4},{4,5},{5,6},{6,7},{7,8},{8,9},{9,10},{10,1... | collective-permute-start | bytes 4718600 | tf_op jit(solution)/shard_map/ppermute | solution.py:11
  123.0 48.4 %collective-permute-start.10 = (s32[384]{0:T(512)S(1)}, s32[384]{0:T(512)S(1)}, u32[]{:S(2)}, u32[]{:S(2)}) collective-permute-start(s32[384]{0:T(512)S(1)} %collective-permute-done.6), channel_id=1, source_target_pairs={{0,1},{1,2},{2,3},{3,4},{4,5},{5,6},{6,7},{7,8},{8,9},{9,10},{10,1... | collective-permute-start | bytes 4616 | tf_op jit(solution)/shard_map/ppermute | solution.py:11
  123.1 60.4 %collective-permute-start.9 = (bf16[384,1024]{1,0:T(8,128)(2,1)S(1)}, bf16[384,1024]{1,0:T(8,128)(2,1)S(1)}, u32[]{:S(2)}, u32[]{:S(2)}) collective-permute-start(bf16[384,1024]{1,0:T(8,128)(2,1)S(1)} %collective-permute-done.5), channel_id=1, source_target_pairs={{0,16},{16,32},{32,48},{48,64},{64,80},{80,96},{96,112},{112,128},... | collective-permute-start | bytes 2359304 | tf_op jit(solution)/shard_map/ppermute | solution.py:11
  171.4 12.1 %collective-permute-start.8 = (s32[384]{0:T(512)S(1)}, s32[384]{0:T(512)S(1)}, u32[]{:S(2)}, u32[]{:S(2)}) collective-permute-start(s32[384]{0:T(512)S(1)} %collective-permute-done.4), channel_id=1, source_target_pairs={{0,16},{16,32},{32,48},{48,64},{64,80},{80,96},{96,112},{112,128},... | collective-permute-start | bytes 4616 | tf_op jit(solution)/shard_map/ppermute | solution.py:11
  185.2 113.3 %collective-permute-start.15 = (f32[384,1024]{1,0:T(8,128)S(1)}, f32[384,1024]{1,0:T(8,128)S(1)}, u32[]{:S(2)}, u32[]{:S(2)}) collective-permute-start(f32[384,1024]{1,0:T(8,128)S(1)} %fusion.37), channel_id=1, source_target_pairs={{0,208},{16,224},{32,240},{48,0},{64,16},{80,32},{96,48},{112,64},... | collective-permute-start | bytes 4718600 | tf_op jit(solution)/shard_map/ppermute | solution.py:11
  266.1 75.2 %collective-permute-start.19 = (f32[384,1024]{1,0:T(8,128)S(1)}, f32[384,1024]{1,0:T(8,128)S(1)}, u32[]{:S(2)}, u32[]{:S(2)}) collective-permute-start(f32[384,1024]{1,0:T(8,128)S(1)} %fusion.40), channel_id=1, source_target_pairs={{0,13},{1,14},{2,15},{3,0},{4,1},{5,2},{6,3},{7,4},{8,5},{9,6},{10... | collective-permute-start | bytes 4718600 | tf_op jit(solution)/shard_map/ppermute | solution.py:11
where the time goes:
time: 344 us
  waiting for transfers between devices  187 us (54%)
  starting transfers between devices  129 us (38%)
  matrix products  21.5 us (6%)
  between operations  3.64 us (1%)
    ppermute x20, waiting for transfers between devices, passed_along(): lax.ppermute(shard, axis, [(i, (i + by) % devices) for i in range(devices)])  187 us
    ppermute x20, starting transfers between devices, passed_along(): lax.ppermute(shard, axis, [(i, (i + by) % devices) for i in range(devices)])  129 us
    dot_general x8, matrix products, weight_tile(): lax.dot_general(video_block, partner, (((1,), (1,)), ((), ())), preferred...  8.5 us
    dot_general x8, matrix products, pair_tile(): video_term = jnp.dot(weighted, partner, preferred_element_type=jnp.float32)  7.41 us
  transfers between devices with their start and end apart: 20, of which 5 were waited for; matrix products, arithmetic and copies ran while one was open for 6% of the time, Pallas kernels for 0%

commit v1 on v0

v1 whole, which is shorter than its diff:
```python
import functools

import jax
import jax.numpy as jnp
from jax import lax
from jax.experimental import pallas as pl
from jax.experimental.pallas import tpu as pltpu
from jax.sharding import PartitionSpec as P

MESH = pl.DeviceIdType.MESH
STEPS = 4
CHUNKS = 3
LANES = 128
TILE = 64

AUDIO, VIDEO_COL, IMU, VIDEO_ROW = range(4)
STREAMS = (AUDIO, VIDEO_COL, IMU, VIDEO_ROW)
MEETS = {AUDIO: VIDEO_COL, VIDEO_COL: AUDIO, IMU: VIDEO_COL, VIDEO_ROW: IMU}
MEETS_IDS = {AUDIO: 0, VIDEO_COL: 2, IMU: 0, VIDEO_ROW: 1}


def kernel(
    n_row,
    n_col,
    video_hbm,
    imu_hbm,
    audio_hbm,
    video_ids,
    imu_ids,
    audio_ids,
    imu_log_scale,
    imu_bias,
    audio_log_scale,
    audio_bias,
    video_grad,
    imu_grad,
    audio_grad,
    row_loss,
    blocks,
    ids,
    columns,
    grads,
    logits,
    weighted,
    losses,
    send_sem,
    recv_sem,
    id_send_sem,
    id_recv_sem,
    load_sem,
    store_sem,
):
    r, c = lax.axis_index("row"), lax.axis_index("col")
    rows = video_hbm.shape[0]
    width = video_hbm.shape[1]
    piece = rows // CHUNKS

    def away(stream, by):
        if stream == AUDIO:
            return (r, lax.rem(c + by + n_col, n_col))
        if stream == VIDEO_COL:
            return (r, lax.rem(c - by + n_col, n_col))
        if stream == IMU:
            return (lax.rem(r + by + n_row, n_row), c)
        return (lax.rem(r - by + n_row, n_row), c)

    own = {AUDIO: audio_hbm, VIDEO_COL: video_hbm, IMU: imu_hbm, VIDEO_ROW: video_hbm}
    own_ids = {AUDIO: audio_ids, VIDEO_COL: video_ids, IMU: imu_ids, VIDEO_ROW: video_ids}

    def travel(stream, slot, k, source):
        return pltpu.make_async_remote_copy(
            src_ref=source,
            dst_ref=blocks.at[stream, slot, pl.ds(k * piece, piece)],
            send_sem=send_sem.at[stream, slot - 1, k],
            recv_sem=recv_sem.at[stream, slot - 1, k],
            device_id=away(stream, 1),
            device_id_type=MESH,
        )

    def travel_ids(stream, slot):
        return pltpu.make_async_remote_copy(
            src_ref=own_ids[stream],
            dst_ref=ids.at[stream, slot],
            send_sem=id_send_sem.at[stream, slot - 1],
            recv_sem=id_recv_sem.at[stream, slot - 1],
            device_id=away(stream, slot),
            device_id_type=MESH,
        )

    barrier = pltpu.get_barrier_semaphore()
    for stream in STREAMS:
        for by in range(1, STEPS):
            pl.semaphore_signal(barrier, inc=1, device_id=away(stream, by), device_id_type=MESH)

    loads = [
        pltpu.make_async_copy(own[stream], blocks.at[stream, 0], load_sem.at[stream])
        for stream in (AUDIO, VIDEO_COL, IMU)
    ]
    for load in loads:
        load.start()

    pl.semaphore_wait(barrier, len(STREAMS) * (STEPS - 1))

    for k in range(CHUNKS):
        for stream in STREAMS:
            travel(stream, 1, k, own[stream].at[pl.ds(k * piece, piece)]).start()
        if k == 0:
            for stream in STREAMS:
                for slot in range(1, STEPS):
                    travel_ids(stream, slot).start()

    groups = rows // LANES
    for entry, ref in enumerate((video_ids, imu_ids, audio_ids)):
        for g in range(groups):
            across = jnp.broadcast_to(ref[g : g + 1, :], (LANES, LANES))
            columns[entry, g * LANES : (g + 1) * LANES, :] = across.T
    for stream in STREAMS:
        ids[stream, 0] = own_ids[stream][...]
    grads[...] = jnp.zeros_like(grads)
    losses[...] = jnp.zeros_like(losses)

    scales = {
        AUDIO: jnp.exp(jnp.full((1, LANES), audio_log_scale[0])),
        IMU: jnp.exp(jnp.full((1, LANES), imu_log_scale[0])),
    }
    offsets = {AUDIO: audio_bias[0], IMU: imu_bias[0]}
    scales[VIDEO_COL], scales[VIDEO_ROW] = scales[AUDIO], scales[IMU]
    offsets[VIDEO_COL], offsets[VIDEO_ROW] = offsets[AUDIO], offsets[IMU]

    def own_block(stream):
        return blocks.at[VIDEO_COL if stream == VIDEO_ROW else stream, 0]

    def meet(stream, partner, first_group, n_groups):
        mine = own_block(MEETS[stream])
        column = columns.at[MEETS_IDS[stream]]
        with_loss = stream in (AUDIO, IMU)
        scale, offset = scales[stream], offsets[stream]
        partner_ids, partner_rows = partner
        span = n_groups * LANES
        logits[:, :span] = lax.dot_general(
            mine[...], partner_rows[...], (((1,), (1,)), ((), ())), preferred_element_type=jnp.float32
        )

        def tile(t, carry):
            at = pl.ds(pl.multiple_of(t * TILE, TILE), TILE)
            tags = column[at, :]
            total = losses[at, :] if with_loss else None
            for g in range(n_groups):
                lanes = slice(g * LANES, (g + 1) * LANES)
                same = tags == partner_ids[pl.ds(first_group + g, 1), :]
                logit = scale * logits[at, lanes] + offset
                z = jnp.where(same, -logit, logit)
                e = jnp.exp(-jnp.abs(z))
                part = 1.0 / (1.0 + e)
                sigmoid = jnp.where(z >= 0.0, part, e * part)
                weighted[at, lanes] = (jnp.where(same, -sigmoid, sigmoid) * scale).astype(jnp.bfloat16)
                if with_loss:
                    total = total + (jnp.maximum(z, 0.0) + jnp.log1p(e))
            if with_loss:
                losses[at, :] = total
            return carry

        lax.fori_loop(0, rows // TILE, tile, 0)
        step = 256
        for n in range(width // step):
            there = slice(n * step, (n + 1) * step)
            grads[stream, :, there] += jnp.dot(
                weighted[:, :span], partner_rows[:, there], preferred_element_type=jnp.float32
            )

    for load in loads:
        load.wait()

    def whole(slot, carry):
        @pl.when(slot > 0)
        def _():
            for k in range(CHUNKS):
                for stream in STREAMS:
                    here = blocks.at[stream, slot, pl.ds(k * piece, piece)]
                    travel(stream, slot, k, here).wait_recv()
                    travel(stream, slot + 1, k, here).start()
            for stream in STREAMS:
                travel_ids_slot(stream, slot).wait_recv()

        for stream in STREAMS:
            source = blocks.at[stream, slot]
            if stream == VIDEO_ROW:
                source = blocks.at[jnp.where(slot == 0, VIDEO_COL, VIDEO_ROW), slot]
            meet(stream, (ids.at[stream, slot], source), 0, groups)
        return carry

    def travel_ids_slot(stream, slot):
        return pltpu.make_async_remote_copy(
            src_ref=own_ids[stream],
            dst_ref=ids.at[stream, slot],
            send_sem=id_send_sem.at[stream, slot - 1],
            recv_sem=id_recv_sem.at[stream, slot - 1],
            device_id=away(stream, 1),
            device_id_type=MESH,
        )

    lax.fori_loop(0, STEPS - 1, whole, 0)

    last = STEPS - 1
    for stream in STREAMS:
        travel_ids(stream, last).wait_recv()

    def pieces(k, carry):
        for stream in (IMU, VIDEO_ROW, AUDIO, VIDEO_COL):
            here = blocks.at[stream, last, pl.ds(k * piece, piece)]
            travel(stream, last, k, here).wait_recv()
            meet(stream, (ids.at[stream, last], here), k * (piece // LANES), piece // LANES)
        return carry

    lax.fori_loop(0, CHUNKS, pieces, 0)

    stores = [
        pltpu.make_async_copy(grads.at[VIDEO_ROW], imu_grad, store_sem.at[0]),
        pltpu.make_async_copy(grads.at[VIDEO_COL], audio_grad, store_sem.at[1]),
        pltpu.make_async_copy(grads.at[AUDIO], video_grad, store_sem.at[2]),
    ]
    stores[0].start()
    stores[1].start()
    grads[AUDIO] += grads[IMU]
    stores[2].start()
    for g in range(groups):
        across = losses[g * LANES : (g + 1) * LANES, :].T
        row_loss[g : g + 1, :] = jnp.sum(across, axis=0, keepdims=True) / (2.0 * STEPS * rows)
    for store in stores:
        store.wait()

    for stream in STREAMS:
        for slot in range(1, STEPS):
            travel_ids(stream, slot).wait_send()
            for k in range(CHUNKS):
                travel(stream, slot, k, blocks.at[stream, slot, pl.ds(k * piece, piece)]).wait_send()


def per_device(n_row, n_col, *args):
    video_rows, video_ids, imu_rows, imu_ids, audio_rows, audio_ids, *scalars = args
    rows, width = video_rows.shape
    groups = rows // LANES
    as_rows = [tags.reshape(groups, LANES) for tags in (video_ids, imu_ids, audio_ids)]
    grad = jax.ShapeDtypeStruct((rows, width), jnp.float32)
    anywhere = pl.BlockSpec(memory_space=pl.ANY)
    vmem = pl.BlockSpec(memory_space=pltpu.VMEM)
    smem = pl.BlockSpec(memory_space=pltpu.SMEM)
    *grads, row_loss = pl.pallas_call(
        functools.partial(kernel, n_row, n_col),
        out_shape=(grad, grad, grad, jax.ShapeDtypeStruct((groups, LANES), jnp.float32)),
        in_specs=[anywhere] * 3 + [vmem] * 3 + [smem] * 4,
        out_specs=(anywhere, anywhere, anywhere, vmem),
        scratch_shapes=[
            pltpu.VMEM((len(STREAMS), STEPS, rows, width), jnp.bfloat16),
            pltpu.VMEM((len(STREAMS), STEPS, groups, LANES), jnp.int32),
            pltpu.VMEM((3, rows, LANES), jnp.int32),
            pltpu.VMEM((len(STREAMS), rows, width), jnp.float32),
            pltpu.VMEM((rows, rows), jnp.float32),
            pltpu.VMEM((rows, rows), jnp.bfloat16),
            pltpu.VMEM((rows, LANES), jnp.float32),
            pltpu.SemaphoreType.DMA((len(STREAMS), STEPS - 1, CHUNKS)),
            pltpu.SemaphoreType.DMA((len(STREAMS), STEPS - 1, CHUNKS)),
            pltpu.SemaphoreType.DMA((len(STREAMS), STEPS - 1)),
            pltpu.SemaphoreType.DMA((len(STREAMS), STEPS - 1)),
            pltpu.SemaphoreType.DMA((3,)),
            pltpu.SemaphoreType.DMA((3,)),
        ],
        compiler_params=pltpu.CompilerParams(
            collective_id=0, has_side_effects=True, vmem_limit_bytes=52 << 20
        ),
    )(video_rows, imu_rows, audio_rows, *as_rows, *scalars)
    return (*grads, row_loss.reshape(rows))


def solution(mesh):
    spread = P(("row", "col"), None)
    flat = P(("row", "col"))
    return jax.shard_map(
        functools.partial(per_device, mesh.shape["row"], mesh.shape["col"]),
        mesh=mesh,
        in_specs=(spread, flat, spread, flat, spread, flat, P(), P(), P(), P()),
        out_specs=(spread, spread, spread, flat),
        check_vma=False,
    )
```

time: 344 us -> 120 us (0.35)
  the two profiles are of different devices: /device:TPU:9 before, /device:TPU:0 now
where the time goes in v1:
time: 120 us; the launch traced here: 118 us
  Pallas kernels  104 us (87%)
  local copies, waits for them, and re-layouts  10.8 us (9%)
  between operations  3.25 us (3%)
    pallas_call x1, Pallas kernels, per_device(): pl.pallas_call(functools.partial(kernel, n_row, n_col), out_shape=(grad,...  104 us
    unnamed x18, local copies, waits for them, and re-layouts  10.8 us

profile of v1, /device:TPU:0, one launch (start us, length us, event | category | flops | bytes accessed | tf_op | source)
XLA Modules:
  0.0 118.4 jit_solution(6759034747784561482)
XLA Ops:
  3.2 0.0 copy-start
  3.2 1.1 copy-done
  4.3 0.0 copy-start.1
  4.4 1.1 copy-done.1
  5.5 0.0 copy-start.2
  5.5 0.7 copy-done.2
  6.2 0.0 copy-start.3
  6.2 0.7 copy-done.3
  6.8 0.0 copy-start.4
  6.8 0.7 copy-done.4
  7.5 104.3 %shard_map.129 = (f32[384,1024]{1,0:T(8,128)}, f32[384,1024]{1,0:T(8,128)}, f32[384,1024]{1,0:T(8,128)}, f32[3,128]{1,0:T(4,128)S(1)}) custom-call(bf16[384,1024]{1,0:T(8,128)(2,1)S(1)} %copy-done, bf16[384,1024]{1,0:T(8,128)(2,1)S(1)} %copy-done.1, bf16[384,1024]{1,0:T(8,128)(2,1)} %audio_hbm.1, s32[3,128]{1,0:T(4,128)S(1)} %bitcast.4, ...), custom_call_target="tpu_custom_call" | custom-call | tf_op jit(solution)/shard_map/pallas_call | solution.py:248
  111.8 0.0 copy-start.6
  111.8 2.8 %copy.22 = f32[384,1024]{1,0:T(8,128)} copy(f32[384,1024]{1,0:T(8,128)} %get-tuple-element.16) | data formatting | bytes 3145728
  114.7 0.0 copy-done.6
  114.7 0.0 copy-start.5
  114.7 1.1 copy.23
  115.8 0.8 copy-done.5
  116.7 1.1 copy.24
  117.8 0.6 copy.25
Async XLA Ops:
  3.2 1.1 copy-start
  4.3 1.1 copy-start.1
  5.5 0.7 copy-start.2
  6.2 0.7 copy-start.3
  6.8 0.7 copy-start.4
  111.8 2.9 %copy-start.6 = (f32[384,1024]{1,0:T(8,128)S(1)}, f32[384,1024]{1,0:T(8,128)}, u32[]{:S(2)}) copy-start(f32[384,1024]{1,0:T(8,128)} %get-tuple-element.17) | copy-start | bytes 4718596
  114.7 2.0 %copy-start.5 = (f32[384,1024]{1,0:T(8,128)S(1)}, f32[384,1024]{1,0:T(8,128)}, u32[]{:S(2)}) copy-start(f32[384,1024]{1,0:T(8,128)} %get-tuple-element.18) | copy-start | bytes 4718596

commit v2 on v1

v2 whole, which is shorter than its diff:
```python
import functools

import jax
import jax.numpy as jnp
from jax import lax
from jax.experimental import pallas as pl
from jax.experimental.pallas import tpu as pltpu
from jax.sharding import PartitionSpec as P

MESH = pl.DeviceIdType.MESH
STEPS = 4
CHUNKS = 3
LANES = 128
TILE = 64
UNROLL = 6
WIDE = 256

AUDIO, VIDEO_COL, IMU, VIDEO_ROW = range(4)
STREAMS = (AUDIO, VIDEO_COL, IMU, VIDEO_ROW)
OWN_VIDEO, OWN_IMU, OWN_AUDIO = range(3)


def kernel(
    n_row,
    n_col,
    video_hbm,
    imu_hbm,
    audio_hbm,
    video_ids,
    imu_ids,
    audio_ids,
    numbers_hbm,
    video_grad,
    imu_grad,
    audio_grad,
    losses,
    own,
    partners,
    videos,
    relay,
    own_ids,
    ids,
    columns,
    logits,
    weighted,
    numbers,
    send_sem,
    recv_sem,
    relay_send_sem,
    relay_recv_sem,
    id_send_sem,
    id_recv_sem,
    load_sem,
    pair_load_sem,
    id_load_sem,
    number_sem,
):
    r, c = lax.axis_index("row"), lax.axis_index("col")
    rows, width = video_hbm.shape
    piece = rows // CHUNKS
    half = n_row // 2
    place_row, place_col = lax.rem(r, half), lax.rem(c, n_col // 2)
    far = n_col // 2 - 1
    edge = jnp.logical_or(place_col == 0, place_col == far)
    near = jnp.logical_or(place_col == 1, place_col == far - 1)
    inward = c + jnp.where(place_col == 0, 1, -1)
    outward = c + jnp.where(place_col == 1, -1, 1)
    both = jnp.logical_and

    def along_row(by):
        return lax.rem(r + by + n_row, n_row)

    def away(stream, by):
        if stream == AUDIO:
            return (r, lax.rem(c + by + n_col, n_col))
        if stream == VIDEO_COL:
            return (r, lax.rem(c - by + n_col, n_col))
        return (along_row(by if stream == IMU else -by), c)

    source_block = {AUDIO: audio_hbm, VIDEO_COL: video_hbm, IMU: imu_hbm, VIDEO_ROW: video_hbm}
    source_ids = {AUDIO: audio_ids, VIDEO_COL: video_ids, IMU: imu_ids, VIDEO_ROW: video_ids}

    def at(k, size=piece):
        return pl.ds(pl.multiple_of(k * size, size), size)

    def landing(stream, slot, k):
        if stream == AUDIO:
            return partners.at[slot, at(2 * k)]
        if stream == IMU:
            return partners.at[slot, at(2 * k + 1)]
        return videos.at[0 if stream == VIDEO_COL else 1, slot - 1, at(k)]

    def remote(source, target, send, recv, device):
        return pltpu.make_async_remote_copy(
            src_ref=source, dst_ref=target, send_sem=send, recv_sem=recv, device_id=device, device_id_type=MESH
        )

    def travel(stream, slot, k, source):
        return remote(
            source,
            landing(stream, slot, k),
            send_sem.at[stream, slot - 1, k],
            recv_sem.at[stream, slot - 1, k],
            away(stream, 1),
        )

    def passes(stream, slot):
        if stream in (AUDIO, VIDEO_COL):
            return None
        at_wrap = place_row == (half - 1 if stream == IMU else 0)
        elsewhere = jnp.logical_or(slot == 3, both(slot == 2, edge))
        return jnp.logical_not(both(at_wrap, elsewhere))

    def when(condition, action):
        if condition is None:
            action()
        else:
            pl.when(condition)(action)

    def travel_ids(stream, slot, by):
        return remote(
            source_ids[stream],
            ids.at[stream, slot],
            id_send_sem.at[stream, slot - 1],
            id_recv_sem.at[stream, slot - 1],
            away(stream, by),
        )

    def relay_copy(leg, source, buffer, k, device):
        return remote(source, relay.at[buffer, at(k)], relay_send_sem.at[leg, k], relay_recv_sem.at[buffer, k], device)

    def relay_last(leg, buffer, stream, slot, k, device):
        return remote(
            relay.at[buffer, at(k)],
            landing(stream, slot, k),
            relay_send_sem.at[leg, k],
            recv_sem.at[stream, slot - 1, k],
            device,
        )

    over = (along_row(half), c)
    third, second = half - 3, half - 2
    leg_0 = (
        (place_row == third, lambda k: relay_copy(0, imu_hbm.at[at(k)], 0, k, over)),
        (place_row == 2, lambda k: relay_copy(0, video_hbm.at[at(k)], 0, k, over)),
        (both(place_row == second, edge), lambda k: relay_copy(2, imu_hbm.at[at(k)], 1, k, (r, inward))),
        (both(place_row == 1, edge), lambda k: relay_copy(2, video_hbm.at[at(k)], 1, k, (r, inward))),
    )
    leg_1 = (
        (place_row == third, lambda k: relay_last(1, 0, IMU, 3, k, (along_row(-third), c))),
        (place_row == 2, lambda k: relay_last(1, 0, VIDEO_ROW, 3, k, (along_row(third), c))),
    )
    leg_1z = (
        (both(jnp.logical_or(place_row == second, place_row == 1), near), lambda k: relay_copy(3, relay.at[1, at(k)], 2, k, over)),
    )
    leg_2z = (
        (both(place_row == second, near), lambda k: relay_last(4, 2, IMU, 2, k, (along_row(-second), outward))),
        (both(place_row == 1, near), lambda k: relay_last(4, 2, VIDEO_ROW, 2, k, (along_row(second), outward))),
    )

    def relay_arrived(buffer, k):
        return remote(relay.at[buffer, at(k)], relay.at[buffer, at(k)], relay_send_sem.at[0, k], relay_recv_sem.at[buffer, k], over)

    barrier = pltpu.get_barrier_semaphore()

    def greet(*device):
        pl.semaphore_signal(barrier, inc=1, device_id=device, device_id_type=MESH)

    for stream in STREAMS:
        for by in range(1, STEPS):
            greet(*away(stream, by))
    count = len(STREAMS) * (STEPS - 1)
    for condition, devices in (
        (place_row == third, (over, (along_row(-third), c))),
        (place_row == 2, (over, (along_row(third), c))),
        (place_row == 0, ((along_row(third), c),)),
        (place_row == half - 1, ((along_row(-third), c),)),
        (both(place_row == second, near), (over, (along_row(-second), outward))),
        (both(place_row == 1, near), (over, (along_row(second), outward))),
        (both(place_row == 0, edge), ((along_row(second), inward),)),
        (both(place_row == half - 1, edge), ((along_row(-second), inward),)),
    ):

        @pl.when(condition)
        def _(devices=devices):
            for device in devices:
                greet(*device)

        count = count + jnp.where(condition, len(devices), 0)

    loads = [
        pltpu.make_async_copy(source, own.at[entry], load_sem.at[entry])
        for entry, source in ((OWN_VIDEO, video_hbm), (OWN_IMU, imu_hbm), (OWN_AUDIO, audio_hbm))
    ]
    for j, (stream, source) in enumerate(((AUDIO, audio_hbm), (IMU, imu_hbm))):
        for k in range(CHUNKS):
            loads.append(pltpu.make_async_copy(source.at[at(k)], landing(stream, 0, k), pair_load_sem.at[j, k]))
    id_loads = [
        pltpu.make_async_copy(source, own_ids.at[entry], id_load_sem.at[entry])
        for entry, source in ((OWN_VIDEO, video_ids), (OWN_IMU, imu_ids), (OWN_AUDIO, audio_ids))
    ]
    id_loads.append(pltpu.make_async_copy(numbers_hbm, numbers, number_sem))
    for load in id_loads + loads:
        load.start()

    pl.semaphore_wait(barrier, count)

    for k in range(CHUNKS):
        for stream in STREAMS:
            travel(stream, 1, k, source_block[stream].at[at(k)]).start()
        for condition, copy in leg_0:
            when(condition, lambda copy=copy: copy(k).start())
        if k == 0:
            for stream in STREAMS:
                for slot in range(1, STEPS):
                    travel_ids(stream, slot, slot).start()

    groups = rows // LANES
    for load in id_loads:
        load.wait()
    for entry in range(3):
        for g in range(groups):
            across = jnp.broadcast_to(own_ids[entry, g : g + 1, :], (LANES, LANES))
            columns[entry, g * LANES : (g + 1) * LANES, :] = across.T
    for stream, entry in ((AUDIO, OWN_AUDIO), (IMU, OWN_IMU), (VIDEO_COL, OWN_VIDEO), (VIDEO_ROW, OWN_VIDEO)):
        ids[stream, 0] = own_ids[entry]
    for grad in (video_grad, imu_grad, audio_grad):
        grad[...] = jnp.zeros_like(grad)
    losses[...] = jnp.zeros_like(losses)

    log_scale_imu, offset_imu, log_scale_audio, offset_audio = (
        jnp.broadcast_to(numbers[:, n : n + 1], (1, LANES)) for n in range(4)
    )
    scale_imu, scale_audio = jnp.exp(log_scale_imu), jnp.exp(log_scale_audio)

    def meet(entry, grad, partner_rows, tags, kinds):
        span = len(kinds) * LANES
        logits[:, :span] = lax.dot_general(
            own[entry], partner_rows[...], (((1,), (1,)), ((), ())), preferred_element_type=jnp.float32
        )
        with_loss = entry == OWN_VIDEO

        def tile(t, carry):
            here = at(t, TILE)
            mine = columns[entry, here, :]
            total = losses[here, :] if with_loss else None
            for g, stream in enumerate(kinds):
                lanes = slice(g * LANES, (g + 1) * LANES)
                by_col = stream in (AUDIO, VIDEO_COL)
                scale, offset = (scale_audio, offset_audio) if by_col else (scale_imu, offset_imu)
                same = mine == tags[g]
                logit = scale * logits[here, lanes] + offset
                z = jnp.where(same, -logit, logit)
                e = jnp.exp(-jnp.abs(logit))
                part = 1.0 / (1.0 + e)
                sigmoid = jnp.where(z >= 0.0, part, e * part)
                weighted[here, lanes] = (jnp.where(same, -sigmoid, sigmoid) * scale).astype(jnp.bfloat16)
                if with_loss:
                    total = total + (jnp.maximum(z, 0.0) + jnp.log1p(e))
            if with_loss:
                losses[here, :] = total
            return carry

        lax.fori_loop(0, rows // TILE, tile, 0, unroll=UNROLL)
        for n in range(width // WIDE):
            there = slice(n * WIDE, (n + 1) * WIDE)
            grad[:, there] += jnp.dot(
                weighted[:, :span], partner_rows[:, there], preferred_element_type=jnp.float32
            )

    def tag(stream, slot, k):
        return ids[stream, slot, pl.ds(k, 1), :]

    def meet_video(slot, ks, partner_rows):
        tags = [tag(stream, slot, k) for k in ks for stream in (AUDIO, IMU)]
        meet(OWN_VIDEO, video_grad, partner_rows, tags, (AUDIO, IMU) * len(ks))

    def meet_partner(stream, slot, ks, video_rows):
        tags = [tag(stream, slot, k) for k in ks]
        if stream == VIDEO_COL:
            meet(OWN_AUDIO, audio_grad, video_rows, tags, (stream,) * len(ks))
        else:
            meet(OWN_IMU, imu_grad, video_rows, tags, (stream,) * len(ks))

    for load in loads:
        load.wait()
    every = range(CHUNKS)
    meet_video(0, every, partners.at[0])
    meet_partner(VIDEO_COL, 0, every, own.at[OWN_VIDEO])
    meet_partner(VIDEO_ROW, 0, every, own.at[OWN_VIDEO])

    def middle(slot, carry):
        for k in every:
            for stream in STREAMS:
                travel(stream, slot, k, landing(stream, slot, k)).wait_recv()
                when(
                    passes(stream, slot + 1),
                    lambda stream=stream: travel(stream, slot + 1, k, landing(stream, slot, k)).start(),
                )
            for step, buffer, legs in ((1, 0, leg_1), (1, 1, leg_1z), (2, 2, leg_2z)):
                for condition, copy in legs:

                    @pl.when(both(condition, slot == step))
                    def _(buffer=buffer, copy=copy):
                        relay_arrived(buffer, k).wait_recv()
                        copy(k).start()

        for stream in STREAMS:
            travel_ids(stream, slot, 1).wait_recv()
        meet_video(slot, every, partners.at[slot])
        for stream in (VIDEO_COL, VIDEO_ROW):
            meet_partner(stream, slot, every, videos.at[0 if stream == VIDEO_COL else 1, slot - 1])
        return carry

    lax.fori_loop(1, STEPS - 1, middle, 0)

    last = STEPS - 1
    for stream in STREAMS:
        travel_ids(stream, last, 1).wait_recv()

    def pieces(k, carry):
        travel(VIDEO_ROW, last, k, landing(VIDEO_ROW, last, k)).wait_recv()
        meet_partner(VIDEO_ROW, last, (k,), landing(VIDEO_ROW, last, k))
        for stream in (IMU, AUDIO):
            travel(stream, last, k, landing(stream, last, k)).wait_recv()
        meet_video(last, (k,), partners.at[last, at(k, 2 * piece)])
        travel(VIDEO_COL, last, k, landing(VIDEO_COL, last, k)).wait_recv()
        meet_partner(VIDEO_COL, last, (k,), landing(VIDEO_COL, last, k))
        return carry

    lax.fori_loop(0, CHUNKS, pieces, 0)

    for stream in STREAMS:
        for slot in range(1, STEPS):
            travel_ids(stream, slot, slot).wait_send()
            for k in range(CHUNKS):
                when(
                    passes(stream, slot),
                    lambda k=k: travel(stream, slot, k, landing(stream, slot, k)).wait_send(),
                )
    for condition, copy in leg_0 + leg_1 + leg_1z + leg_2z:

        @pl.when(condition)
        def _(copy=copy):
            for k in range(CHUNKS):
                copy(k).wait_send()


def write_out(
    pairs, video_in, imu_in, audio_in, losses, video_out, imu_out, audio_out, loss_out, row_loss, store_sem, loss_sem
):
    stores = [
        pltpu.make_async_copy(source, target, store_sem.at[n])
        for n, (source, target) in enumerate(((video_in, video_out), (imu_in, imu_out), (audio_in, audio_out)))
    ]
    for store in stores:
        store.start()
    for g in range(losses.shape[0] // LANES):
        across = losses[g * LANES : (g + 1) * LANES, :].T
        row_loss[g : g + 1, :] = jnp.sum(across, axis=0, keepdims=True) / pairs
    store = pltpu.make_async_copy(row_loss, loss_out, loss_sem)
    store.start()
    for store in stores + [store]:
        store.wait()


def per_device(n_row, n_col, *args):
    video_rows, video_ids, imu_rows, imu_ids, audio_rows, audio_ids, *scalars = args
    rows, width = video_rows.shape
    groups = rows // LANES
    as_rows = [tags.reshape(groups, LANES) for tags in (video_ids, imu_ids, audio_ids)]
    numbers = jnp.concatenate(scalars).reshape(1, len(scalars))
    operands = (video_rows, imu_rows, audio_rows, *as_rows, numbers)
    grad = jax.ShapeDtypeStruct((rows, width), jnp.float32)
    hbm = pl.BlockSpec(memory_space=pltpu.HBM)
    vmem = pl.BlockSpec(memory_space=pltpu.VMEM)
    dma = pltpu.SemaphoreType.DMA
    sums = pl.pallas_call(
        functools.partial(kernel, n_row, n_col),
        out_shape=(grad, grad, grad, jax.ShapeDtypeStruct((rows, LANES), jnp.float32)),
        in_specs=[hbm] * 7,
        out_specs=(vmem,) * 4,
        scratch_shapes=[
            pltpu.VMEM((3, rows, width), jnp.bfloat16),
            pltpu.VMEM((STEPS, 2 * rows, width), jnp.bfloat16),
            pltpu.VMEM((2, STEPS - 1, rows, width), jnp.bfloat16),
            pltpu.VMEM((3, rows, width), jnp.bfloat16),
            pltpu.VMEM((3, groups, LANES), jnp.int32),
            pltpu.VMEM((len(STREAMS), STEPS, groups, LANES), jnp.int32),
            pltpu.VMEM((3, rows, LANES), jnp.int32),
            pltpu.VMEM((rows, 2 * rows), jnp.float32),
            pltpu.VMEM((rows, 2 * rows), jnp.bfloat16),
            pltpu.VMEM((1, 4), jnp.float32),
            dma((len(STREAMS), STEPS - 1, CHUNKS)),
            dma((len(STREAMS), STEPS - 1, CHUNKS)),
            dma((5, CHUNKS)),
            dma((3, CHUNKS)),
            dma((len(STREAMS), STEPS - 1)),
            dma((len(STREAMS), STEPS - 1)),
            dma((3,)),
            dma((2, CHUNKS)),
            dma((3,)),
            dma,
        ],
        compiler_params=pltpu.CompilerParams(
            collective_id=0, has_side_effects=True, vmem_limit_bytes=40 << 20
        ),
    )(*(pltpu.with_memory_space_constraint(operand, pltpu.HBM) for operand in operands))
    *grads, row_loss = pl.pallas_call(
        functools.partial(write_out, 2.0 * STEPS * rows),
        out_shape=(grad, grad, grad, jax.ShapeDtypeStruct((groups, LANES), jnp.float32)),
        in_specs=[vmem] * 4,
        out_specs=(hbm,) * 4,
        scratch_shapes=[pltpu.VMEM((groups, LANES), jnp.float32), dma((3,)), dma],
        compiler_params=pltpu.CompilerParams(vmem_limit_bytes=4 << 20),
    )(*sums)
    return (*grads, row_loss.reshape(rows))


def solution(mesh):
    spread = P(("row", "col"), None)
    flat = P(("row", "col"))
    return jax.shard_map(
        functools.partial(per_device, mesh.shape["row"], mesh.shape["col"]),
        mesh=mesh,
        in_specs=(spread, flat, spread, flat, spread, flat, P(), P(), P(), P()),
        out_specs=(spread, spread, spread, flat),
        check_vma=False,
    )
```

time: 120 us -> 95.8 us (0.80); the launches traced: 118 us -> 95.7 us
  Pallas kernels: 104 us -> 91.9 us
  local copies, waits for them, and re-layouts: 10.8 us -> 0 us
    pallas_call x1, Pallas kernels: 104 us -> 89.7 us  [per_device(): pl.pallas_call(functools.partial(kernel, n_row, n_col), out_shape=(grad,...]
    unnamed x18 -> x0, local copies, waits for them, and re-layouts: 10.8 us -> none
    pallas_call x0 -> x1, Pallas kernels: none -> 2.22 us  [per_device(): pl.pallas_call(functools.partial(write_out, 2.0 * STEPS * rows), out_shap...]
where the time goes in v2:
time: 95.8 us; the launch traced here: 95.7 us
  Pallas kernels  91.9 us (96%)
  between operations  3.22 us (3%)
    pallas_call x1, Pallas kernels, per_device(): pl.pallas_call(functools.partial(kernel, n_row, n_col), out_shape=(grad,...  89.7 us
    pallas_call x1, Pallas kernels, per_device(): pl.pallas_call(functools.partial(write_out, 2.0 * STEPS * rows), out_shap...  2.22 us

profile of v2, /device:TPU:0, one launch (start us, length us, event | category | flops | bytes accessed | tf_op | source)
XLA Modules:
  0.0 95.7 jit_solution(13089585410468104120)
XLA Ops:
  3.2 0.6 maximum_bitcast_fusion.numbers_hbm
  3.8 89.7 %shard_map.129 = (f32[384,1024]{1,0:T(8,128)S(1)}, f32[384,1024]{1,0:T(8,128)S(1)}, f32[384,1024]{1,0:T(8,128)S(1)}, f32[384,128]{1,0:T(8,128)S(1)}) custom-call(bf16[384,1024]{1,0:T(8,128)(2,1)} %video_hbm.1, bf16[384,1024]{1,0:T(8,128)(2,1)} %imu_hbm.1, bf16[384,1024]{1,0:T(8,128)(2,1)} %audio_hbm.1, s32[3,128]{1,0:T(4,128)} %bitcast.6, s32[3,128]{1,0:T(4,128)} %bitcast.7, ...), custom_call_target="tpu_custom_call" | custom-call | tf_op jit(solution)/shard_map/pallas_call | solution.py:378
  93.5 2.2 %shard_map.130 = (f32[384,1024]{1,0:T(8,128)}, f32[384,1024]{1,0:T(8,128)}, f32[384,1024]{1,0:T(8,128)}, f32[3,128]{1,0:T(4,128)}) custom-call(f32[384,1024]{1,0:T(8,128)S(1)} %get-tuple-element.12.video_in, f32[384,1024]{1,0:T(8,128)S(1)} %get-tuple-element.13.imu_in, f32[384,1024]{1,0:T(8,128)S(1)} %get-tuple-element.14.audio_in, ...), custom_call_target="tpu_custom_call" | custom-call | tf_op jit(solution)/shard_map/pallas_call | solution.py:409

commit v3 on v2

--- a/solution.py
+++ b/solution.py
@@ -17,6 +17,8 @@
 
 AUDIO, VIDEO_COL, IMU, VIDEO_ROW = range(4)
 STREAMS = (AUDIO, VIDEO_COL, IMU, VIDEO_ROW)
+ORDER = (AUDIO, VIDEO_COL, IMU, VIDEO_ROW)
+START_Z1, START_Z2, START_Y = 0, 2, 4
 OWN_VIDEO, OWN_IMU, OWN_AUDIO = range(3)
 
 
@@ -206,7 +208,10 @@
     pl.semaphore_wait(barrier, count)
 
     for k in range(CHUNKS):
-        for stream in STREAMS:
+        for stream in (IMU, VIDEO_ROW):
+            travel(stream, 1, k, source_block[stream].at[at(k)]).start()
+    for k in range(CHUNKS):
+        for stream in (AUDIO, VIDEO_COL):
             travel(stream, 1, k, source_block[stream].at[at(k)]).start()
         for condition, copy in leg_0:
             when(condition, lambda copy=copy: copy(k).start())
@@ -289,46 +294,34 @@
     meet_partner(VIDEO_COL, 0, every, own.at[OWN_VIDEO])
     meet_partner(VIDEO_ROW, 0, every, own.at[OWN_VIDEO])
 
-    def middle(slot, carry):
-        for k in every:
+    def step(t, carry):
+        slot, k = 1 + t // CHUNKS, lax.rem(t, CHUNKS)
+        for stream in ORDER:
+            travel(stream, slot, k, landing(stream, slot, k)).wait_recv()
+            onward = slot < STEPS - 1
+            allowed = passes(stream, slot + 1)
+            pl.when(onward if allowed is None else both(onward, allowed))(
+                lambda stream=stream: travel(stream, slot + 1, k, landing(stream, slot, k)).start()
+            )
+        for start, buffer, legs in ((START_Y, 0, leg_1), (START_Z1, 1, leg_1z), (START_Z2, 2, leg_2z)):
+            for condition, copy in legs:
+
+                @pl.when(both(condition, both(t >= start, t < start + CHUNKS)))
+                def _(start=start, buffer=buffer, copy=copy):
+                    relay_arrived(buffer, t - start).wait_recv()
+                    copy(t - start).start()
+
+        @pl.when(k == 0)
+        def _():
             for stream in STREAMS:
-                travel(stream, slot, k, landing(stream, slot, k)).wait_recv()
-                when(
-                    passes(stream, slot + 1),
-                    lambda stream=stream: travel(stream, slot + 1, k, landing(stream, slot, k)).start(),
-                )
-            for step, buffer, legs in ((1, 0, leg_1), (1, 1, leg_1z), (2, 2, leg_2z)):
-                for condition, copy in legs:
-
-                    @pl.when(both(condition, slot == step))
-                    def _(buffer=buffer, copy=copy):
-                        relay_arrived(buffer, k).wait_recv()
-                        copy(k).start()
-
-        for stream in STREAMS:
-            travel_ids(stream, slot, 1).wait_recv()
-        meet_video(slot, every, partners.at[slot])
-        for stream in (VIDEO_COL, VIDEO_ROW):
-            meet_partner(stream, slot, every, videos.at[0 if stream == VIDEO_COL else 1, slot - 1])
+                travel_ids(stream, slot, 1).wait_recv()
+
+        meet_video(slot, (k,), partners.at[slot, at(k, 2 * piece)])
+        meet_partner(VIDEO_COL, slot, (k,), landing(VIDEO_COL, slot, k))
+        meet_partner(VIDEO_ROW, slot, (k,), landing(VIDEO_ROW, slot, k))
         return carry
 
-    lax.fori_loop(1, STEPS - 1, middle, 0)
-
-    last = STEPS - 1
-    for stream in STREAMS:
-        travel_ids(stream, last, 1).wait_recv()
-
-    def pieces(k, carry):
-        travel(VIDEO_ROW, last, k, landing(VIDEO_ROW, last, k)).wait_recv()
-        meet_partner(VIDEO_ROW, last, (k,), landing(VIDEO_ROW, last, k))
-        for stream in (IMU, AUDIO):
-            travel(stream, last, k, landing(stream, last, k)).wait_recv()
-        meet_video(last, (k,), partners.at[last, at(k, 2 * piece)])
-        travel(VIDEO_COL, last, k, landing(VIDEO_COL, last, k)).wait_recv()
-        meet_partner(VIDEO_COL, last, (k,), landing(VIDEO_COL, last, k))
-        return carry
-
-    lax.fori_loop(0, CHUNKS, pieces, 0)
+    lax.fori_loop(0, CHUNKS * (STEPS - 1), step, 0)
 
     for stream in STREAMS:
         for slot in range(1, STEPS):

time: 95.8 us -> 89.9 us (0.938); the launches traced: 95.7 us -> 88.5 us
  Pallas kernels: 91.9 us -> 84.7 us
    pallas_call x1, Pallas kernels: 89.7 us -> 82.5 us  [per_device(): pl.pallas_call(functools.partial(kernel, n_row, n_col), out_shape=(grad,...]
where the time goes in v3:
time: 89.9 us; the launch traced here: 88.5 us
  Pallas kernels  84.7 us (94%)
  between operations  3.22 us (4%)
    pallas_call x1, Pallas kernels, per_device(): pl.pallas_call(functools.partial(kernel, n_row, n_col), out_shape=(grad,...  82.5 us
    pallas_call x1, Pallas kernels, per_device(): pl.pallas_call(functools.partial(write_out, 2.0 * STEPS * rows), out_shap...  2.22 us

profile of v3, /device:TPU:0, one launch (start us, length us, event | category | flops | bytes accessed | tf_op | source)
XLA Modules:
  0.0 88.5 jit_solution(14522462271963751418)
XLA Ops:
  3.2 0.6 maximum_bitcast_fusion.numbers_hbm
  3.8 82.5 %shard_map.129 = (f32[384,1024]{1,0:T(8,128)S(1)}, f32[384,1024]{1,0:T(8,128)S(1)}, f32[384,1024]{1,0:T(8,128)S(1)}, f32[384,128]{1,0:T(8,128)S(1)}) custom-call(bf16[384,1024]{1,0:T(8,128)(2,1)} %video_hbm.1, bf16[384,1024]{1,0:T(8,128)(2,1)} %imu_hbm.1, bf16[384,1024]{1,0:T(8,128)(2,1)} %audio_hbm.1, s32[3,128]{1,0:T(4,128)} %bitcast.6, s32[3,128]{1,0:T(4,128)} %bitcast.7, ...), custom_call_target="tpu_custom_call" | custom-call | tf_op jit(solution)/shard_map/pallas_call | solution.py:371
  86.3 2.2 %shard_map.130 = (f32[384,1024]{1,0:T(8,128)}, f32[384,1024]{1,0:T(8,128)}, f32[384,1024]{1,0:T(8,128)}, f32[3,128]{1,0:T(4,128)}) custom-call(f32[384,1024]{1,0:T(8,128)S(1)} %get-tuple-element.12.video_in, f32[384,1024]{1,0:T(8,128)S(1)} %get-tuple-element.13.imu_in, f32[384,1024]{1,0:T(8,128)S(1)} %get-tuple-element.14.audio_in, ...), custom_call_target="tpu_custom_call" | custom-call | tf_op jit(solution)/shard_map/pallas_call | solution.py:402

commit v4 on v3

--- a/solution.py
+++ b/solution.py
@@ -210,11 +210,11 @@
     for k in range(CHUNKS):
         for stream in (IMU, VIDEO_ROW):
             travel(stream, 1, k, source_block[stream].at[at(k)]).start()
+        for condition, copy in leg_0:
+            when(condition, lambda copy=copy: copy(k).start())
     for k in range(CHUNKS):
         for stream in (AUDIO, VIDEO_COL):
             travel(stream, 1, k, source_block[stream].at[at(k)]).start()
-        for condition, copy in leg_0:
-            when(condition, lambda copy=copy: copy(k).start())
         if k == 0:
             for stream in STREAMS:
                 for slot in range(1, STEPS):

time: 89.9 us -> 89 us (0.990)
  the two profiles are of different devices: /device:TPU:0 before, /device:TPU:32 now
where the time goes in v4:
time: 89 us; the launch traced here: 88.8 us
  Pallas kernels  85 us (96%)
  between operations  3.22 us (4%)
    pallas_call x1, Pallas kernels, per_device(): pl.pallas_call(functools.partial(kernel, n_row, n_col), out_shape=(grad,...  82.8 us
    pallas_call x1, Pallas kernels, per_device(): pl.pallas_call(functools.partial(write_out, 2.0 * STEPS * rows), out_shap...  2.22 us

profile of v4, /device:TPU:32, one launch (start us, length us, event | category | flops | bytes accessed | tf_op | source)
XLA Modules:
  0.0 88.8 jit_solution(14952807473434300006)
XLA Ops:
  3.2 0.6 maximum_bitcast_fusion.numbers_hbm
  3.8 82.8 %shard_map.129 = (f32[384,1024]{1,0:T(8,128)S(1)}, f32[384,1024]{1,0:T(8,128)S(1)}, f32[384,1024]{1,0:T(8,128)S(1)}, f32[384,128]{1,0:T(8,128)S(1)}) custom-call(bf16[384,1024]{1,0:T(8,128)(2,1)} %video_hbm.1, bf16[384,1024]{1,0:T(8,128)(2,1)} %imu_hbm.1, bf16[384,1024]{1,0:T(8,128)(2,1)} %audio_hbm.1, s32[3,128]{1,0:T(4,128)} %bitcast.6, s32[3,128]{1,0:T(4,128)} %bitcast.7, ...), custom_call_target="tpu_custom_call" | custom-call | tf_op jit(solution)/shard_map/pallas_call | solution.py:371
  86.6 2.2 %shard_map.130 = (f32[384,1024]{1,0:T(8,128)}, f32[384,1024]{1,0:T(8,128)}, f32[384,1024]{1,0:T(8,128)}, f32[3,128]{1,0:T(4,128)}) custom-call(f32[384,1024]{1,0:T(8,128)S(1)} %get-tuple-element.12.video_in, f32[384,1024]{1,0:T(8,128)S(1)} %get-tuple-element.13.imu_in, f32[384,1024]{1,0:T(8,128)S(1)} %get-tuple-element.14.audio_in, ...), custom_call_target="tpu_custom_call" | custom-call | tf_op jit(solution)/shard_map/pallas_call | solution.py:402
